TPU v7x, 256 devices: a whole 4x4x8 slice. The times are simulated.
256 devices in a mesh: dp: 8 (over y, z_hi), mp: 32 (over z_lo, x, core).
Axes of the slice: x: 4, y: 4, z: 8 (z_hi: 2, z_lo: 4; z = z_hi * 4 + z_lo), core: 2. Of those that a mesh axis runs over, the one named last changes fastest.
Arguments:
- features: bfloat16 [256, 1280, 1024], P('dp', 'mp'), may hold values from -6 to 6
- conv_weight: bfloat16 [1280, 1280], P('mp'), may hold values from -0.15625 to 0.15625
- norm_gain: float32 [1280], replicated, may hold values from 0.25 to 1.75
- norm_bias: float32 [1280], replicated, may hold values from -3 to 3
- logit_vector: float32 [1280], replicated, may hold values from -0.625 to 0.625
- labels: int32 [256], P(('dp', 'mp')), may hold values 0 or 1
Outputs:
- grad_features: float32 [256, 1280, 1024], P('dp', 'mp')
- grad_weight: float32 [1280, 1280], P('mp')
- head_grads: float32 [3, 1280], replicated
- loss: float32 [], replicated
All inputs are finite; a program needn't handle non-finite values. No bound on the sum of `labels` on one device may be relied on, other than what follows from the above.
Results may differ from a plain program's by a relative error of at most 0.0029.
Values may be sent and summed in bfloat16 or wider, within the bound.
A program may use at most 128 MiB of HBM per device.

v0:
```python
import functools

import jax
import jax.numpy as jnp
from jax import lax
from jax.sharding import Mesh
from jax.sharding import PartitionSpec as P

GROUPS = 32
MP = ("mp_0", "mp_1", "mp_2")
DP = ("dp_0", "dp_1")
DP_MP = ("dp_0", "dp_1", "mp_0", "mp_1", "mp_2")


norm_eps = 1e-05


def from_everyone(x, axis):
    copies = jnp.broadcast_to(x, (lax.axis_size(axis), *x.shape))
    return lax.all_to_all(copies, axis, split_axis=0, concat_axis=0, tiled=True)


def taken_together(x, axis):
    return from_everyone(x, axis).sum(axis=0)


def by_axis(x, axes):
    return functools.reduce(lax.psum, axes, x)


def head_total(pre, norm_gain, norm_bias, logit_vector, signs):
    images, channels, cell_count = pre.shape
    grouped = pre.reshape(images, GROUPS, channels // GROUPS, cell_count)
    center = jnp.mean(grouped, axis=(2, 3), keepdims=True)
    spread = jnp.mean((grouped - center) ** 2, axis=(2, 3), keepdims=True)
    normed = ((grouped - center) * lax.rsqrt(spread + norm_eps)).reshape(
        images, channels, cell_count
    )
    normed = normed * norm_gain[:, None] + norm_bias[:, None]
    hidden = jax.nn.silu(normed)
    logits = (
        jnp.einsum("c,ncs->n", logit_vector, hidden, precision=lax.Precision.HIGHEST) / cell_count
    )
    margin = jnp.maximum(1.0 - signs * logits, 0.0)
    return jnp.sum(margin * margin)


def shards(features, conv_weight, norm_gain, norm_bias, logit_vector, labels):
    signs = 2.0 * labels.astype(jnp.float32) - 1.0
    weight_full = lax.all_gather(conv_weight, MP, axis=0, tiled=True)
    image_block = lax.all_to_all(features, MP, split_axis=0, concat_axis=1, tiled=True)
    pre = jnp.einsum("io,nis->nos", weight_full, image_block, preferred_element_type=jnp.float32)
    total, pull = jax.vjp(
        lambda p, g, b, h: head_total(p, g, b, h, signs), pre, norm_gain, norm_bias, logit_vector
    )
    grad_pre, grad_gain, grad_bias, grad_vec = pull(jnp.ones((), jnp.float32))
    grad_pre = grad_pre.astype(jnp.bfloat16)
    grad_image = jnp.einsum(
        "io,nos->nis", weight_full, grad_pre, preferred_element_type=jnp.float32
    )
    grad_features = lax.all_to_all(grad_image, MP, split_axis=1, concat_axis=0, tiled=True)
    weight_term = jnp.einsum(
        "nis,nos->io", image_block, grad_pre, preferred_element_type=jnp.float32
    )
    weight_rows = lax.psum_scatter(weight_term, MP, scatter_dimension=0, tiled=True)
    grad_weight = taken_together(weight_rows, DP)
    total_sum, head_grads = (
        by_axis(total, DP_MP),
        by_axis(jnp.stack([grad_gain, grad_bias, grad_vec]), DP_MP),
    )
    image_total = pre.shape[0] * lax.axis_size(DP) * lax.axis_size(MP)
    loss = total_sum / image_total
    return (grad_features, grad_weight, head_grads, loss)


def solution(mesh):
    finer = Mesh(mesh.devices.reshape(4, 2, 4, 4, 2), ("dp_0", "dp_1", "mp_0", "mp_1", "mp_2"))
    placed = (P(DP, MP, None), P(MP, None), P(), P(), P(), P(DP_MP))
    return jax.shard_map(
        shards,
        mesh=finer,
        in_specs=placed,
        out_specs=(P(DP, MP, None), P(MP, None), P(), P()),
        check_vma=False,
    )
```

profile of v0, /device:TPU:6, one launch (start us, length us, event | category | flops | bytes accessed | tf_op | source)
XLA Modules:
  0.0 427.4 jit_solution(11983698278212460681)
XLA Ops:
  7.2 0.0 all-gather.2.cloned.1.call-start
  7.2 0.7 all-gather.2.cloned.1.call-update
  7.9 9.0 %all-to-all-start = ((bf16[32,40,1024]{2,1,0:T(8,128)(2,1)}), bf16[32,40,1024]{2,1,0:T(8,128)(2,1)S(1)}, u32[]{:S(2)}, u32[]{:S(2)}) async-start(bf16[32,40,1024]{2,1,0:T(8,128)(2,1)} %param.6), calls=%async_computation | async-start | bytes 5242880 | tf_op jit(solution)/shard_map/all_to_all | solution.py:51
  16.9 0.0 reduce-scatter.4.cloned.1.call-start
  17.6 72.1 %all-to-all-done = bf16[32,40,1024]{2,1,0:T(8,128)(2,1)S(1)} async-done(((bf16[32,40,1024]{2,1,0:T(8,128)(2,1)}), bf16[32,40,1024]{2,1,0:T(8,128)(2,1)S(1)}, u32[]{:S(2)}, u32[]{:S(2)}) %all-to-all-start) | async-done | bytes 2621472 | tf_op jit(solution)/shard_map/all_to_all | solution.py:51
  89.7 4.6 %all-gather.2.cloned.1.call-done = bf16[1280,1280]{1,0:T(8,128)(2,1)} async-done(((bf16[40,1280]{1,0:T(8,128)(2,1)}), bf16[1280,1280]{1,0:T(8,128)(2,1)}) %all-gather.2.cloned.1.call-update) | async-done | bytes 3276816 | tf_op jit(solution)/shard_map/all_gather | solution.py:50
  94.3 7.3 %fusion.10 = (f32[1280]{0:T(1024)S(1)}, f32[1024,1280]{1,0:T(8,128)}) fusion(bf16[1280,1024]{1,0:T(8,128)(2,1)S(1)} %bitcast.86, bf16[1280,1280]{1,0:T(8,128)(2,1)} %all-gather.2.cloned.1.call-done), kind=kOutput, calls=%fused_computation.30 | convolution fusion | flops 3356752640 | bytes 11146240 | tf_op jit(solution)/shard_map/io,nis->nos/dot_general | solution.py:52
  101.6 0.1 reduce_sum.147
  101.7 0.1 reduce_sum.148
  101.9 0.1 sub.52
  101.9 0.1 sub.53
  102.0 0.0 copy-start.2
  102.0 3.1 fusion.2
  105.1 0.1 reduce_sum.150
  105.2 0.1 reduce_sum.151
  105.3 0.1 mul.155
  105.4 0.1 mul.156
  105.5 0.0 copy-done
  105.5 4.2 multiply_reduce_fusion.1
  109.7 0.6 multiply_reduce_fusion.3
  111.0 5.7 %multiply_reduce_fusion = (f32[1280]{0:T(1024)S(1)}, f32[1280]{0:T(1024)S(1)}, f32[1280]{0:T(1024)S(1)}, f32[1280]{0:T(1024)S(1)}) fusion(f32[1024,1280]{1,0:T(8,128)} %get-tuple-element.23, f32[1280]{0:T(1024)S(1)} %mul.156, f32[1280]{0:T(1024)S(1)} %sub.53, f32[1280]{0:T(1024)S(1)} %copy-done, f32[1280]{0:T(1024)S(1)} %copy-done.1, ...), kind=kLoop, calls=%fused_computation.11 | loop fusion | flops 27520000 | bytes 5288960 | tf_op jit(solution)/shard_map/transpose(jvp())/reduce_sum | solution.py:39
  116.7 0.1 reduce_sum.157
  116.8 0.1 reduce_sum.158
  116.9 0.1 reduce_sum.154
  117.0 0.1 reduce_sum.155
  117.2 0.1 mul.177
  117.2 0.1 mul.178
  117.3 3.1 fusion.4
  120.4 0.1 reduce_sum.160
  120.5 0.1 reduce_sum.161
  120.6 0.1 broadcast_in_dim.11
  120.7 0.1 broadcast_in_dim.24
  120.8 11.6 %convolution_bitcast_fusion = f32[1280,1280]{0,1:T(8,128)} fusion(bf16[1280,1024]{1,0:T(8,128)(2,1)S(1)} %bitcast.87, f32[1024,1280]{1,0:T(8,128)} %get-tuple-element.23, f32[1280]{0:T(1024)S(1)} %broadcast_in_dim.24, f32[1280]{0:T(1024)S(1)} %mul.178, f32[1280]{0:T(1024)S(1)} %copy-done.1, f32[1280]{0:T(1024)S(1)} %mul.156, f32[1280]{0:T(1024)S(1)} %sub.53, ...), kind=kOutput, calls=%fused_computation | convolution fusion | flops 3380346880 | bytes 14453760 | tf_op jit(solution)/shard_map/nis,nos->io/dot_general | solution.py:62
  132.4 8.2 %copy.20 = f32[1280,1280]{1,0:T(8,128)} copy(f32[1280,1280]{0,1:T(8,128)} %convolution_bitcast_fusion) | data formatting | bytes 13107200
  140.6 0.0 reduce-scatter.4.cloned.1.call-update
  140.6 12.1 %convolution_bitcast_fusion.1 = f32[1,1280,1024]{1,2,0:T(8,128)} fusion(bf16[1280,1280]{1,0:T(8,128)(2,1)} %all-gather.2.cloned.1.call-done, f32[1024,1280]{1,0:T(8,128)} %get-tuple-element.23, f32[1280]{0:T(1024)S(1)} %broadcast_in_dim.24, f32[1280]{0:T(1024)S(1)} %mul.178, f32[1280]{0:T(1024)S(1)} %copy-done.1, f32[1280]{0:T(1024)S(1)} %mul.156, ...), kind=kOutput, calls=%fused_computation.18 | convolution fusion | flops 3380346880 | bytes 13798400 | tf_op jit(solution)/shard_map/io,nos->nis/dot_general | solution.py:58
  152.7 11.6 %copy.16 = f32[1,1280,1024]{2,0,1:T(1,128)} copy(f32[1,1280,1024]{1,2,0:T(8,128)} %convolution_bitcast_fusion.1) | data formatting | bytes 10485760 | tf_op jit(solution)/shard_map/io,nos->nis/transpose | solution.py:58
  164.3 152.4 %all_to_all.26 = f32[1,1280,1024]{2,0,1:T(1,128)} all-to-all(f32[1,1280,1024]{2,0,1:T(1,128)} %copy.16), channel_id=1, replica_groups=mesh['dp_0'=4,'dp_1'=2,'mp_0'=4,'mp_1'=4,'mp_2'=2] {'mp_0','mp_1','mp_2'}, dimensions={1} | all-to-all | bytes 10485760 | tf_op jit(solution)/shard_map/all_to_all | solution.py:61
  316.7 2.2 broadcast_in_dim.26
  318.9 7.6 %all-to-all-start.2 = ((f32[8,40,1280]{2,1,0:T(8,128)}), f32[8,40,1280]{2,1,0:T(8,128)S(1)}, u32[]{:S(2)}, u32[]{:S(2)}) async-start(f32[8,40,1280]{2,1,0:T(8,128)} %broadcast_in_dim.26), calls=%async_computation.2 | async-start | bytes 3276800 | tf_op jit(solution)/shard_map/all_to_all | solution.py:20
  326.6 21.4 %all-reduce.2 = (f32[3,1280]{1,0:T(4,128)S(1)}, f32[]{:T(128)}) all-reduce(f32[3,1280]{1,0:T(4,128)S(1)} %pad_maximum_fusion, f32[]{:T(128)} %bitcast.9), channel_id=1, replica_groups=mesh['dp_0'=4,'dp_1'=2,'mp_0'=4,'mp_1'=4,'mp_2'=2] {'dp_0'}, use_global_device_ids=true, to_apply=%region_15.16 | all-reduce | flops 3841 | bytes 30728 | tf_op jit(solution)/shard_map/psum | solution.py:28
  348.0 22.8 %all-reduce.4 = (f32[3,1280]{1,0:T(4,128)S(1)}, f32[]{:T(128)}) all-reduce(f32[3,1280]{1,0:T(4,128)S(1)} %get-tuple-element.16, f32[]{:T(128)} %get-tuple-element.17), channel_id=1, replica_groups=mesh['dp_0'=4,'dp_1'=2,'mp_0'=4,'mp_1'=4,'mp_2'=2] {'dp_1'}, use_global_device_ids=true, to_apply=%region_16.17 | all-reduce | flops 3841 | bytes 30728 | tf_op jit(solution)/shard_map/psum | solution.py:28
  370.8 21.4 %all-reduce.1 = (f32[3,1280]{1,0:T(4,128)S(1)}, f32[]{:T(128)}) all-reduce(f32[3,1280]{1,0:T(4,128)S(1)} %get-tuple-element.20, f32[]{:T(128)} %get-tuple-element.21), channel_id=1, replica_groups=mesh['dp_0'=4,'dp_1'=2,'mp_0'=4,'mp_1'=4,'mp_2'=2] {'mp_0'}, use_global_device_ids=true, to_apply=%region_17.18 | all-reduce | flops 3841 | bytes 30728 | tf_op jit(solution)/shard_map/psum | solution.py:28
  392.2 15.1 %all-reduce = (f32[3,1280]{1,0:T(4,128)S(1)}, f32[]{:T(128)}) all-reduce(f32[3,1280]{1,0:T(4,128)S(1)} %get-tuple-element.14, f32[]{:T(128)} %get-tuple-element.15), channel_id=1, replica_groups=mesh['dp_0'=4,'dp_1'=2,'mp_0'=4,'mp_1'=4,'mp_2'=2] {'mp_1'}, use_global_device_ids=true, to_apply=%region_18.19 | all-reduce | flops 3841 | bytes 30728 | tf_op jit(solution)/shard_map/psum | solution.py:28
  407.3 4.6 %all-reduce.3 = (f32[3,1280]{1,0:T(4,128)}, f32[]{:T(128)}) all-reduce(f32[3,1280]{1,0:T(4,128)S(1)} %get-tuple-element.12, f32[]{:T(128)} %get-tuple-element.13), channel_id=1, replica_groups=mesh['dp_0'=4,'dp_1'=2,'mp_0'=4,'mp_1'=4,'mp_2'=2] {'mp_2'}, use_global_device_ids=true, to_apply=%region_19.20 | all-reduce | flops 3841 | bytes 30728 | tf_op jit(solution)/shard_map/psum | solution.py:28
  412.5 6.1 %copy.22 = f32[1,1280,1024]{2,1,0:T(8,128)} copy(f32[1,1280,1024]{2,0,1:T(1,128)} %all_to_all.26) | data formatting | bytes 10485760
  418.6 0.0 all-to-all-done.2
  418.6 0.8 reduce_sum.162
  (15 shorter events, 0.1 us)
Async XLA Ops:
  7.2 87.2 %all-gather.2.cloned.1.call-start = ((), (), s32[]{:S(2)}) async-start(), calls=%async_computation.4 | async-start | bytes 3379200 | tf_op jit(solution)/shard_map/all_gather | solution.py:50
  7.9 81.8 %all-to-all-start = ((bf16[32,40,1024]{2,1,0:T(8,128)(2,1)}), bf16[32,40,1024]{2,1,0:T(8,128)(2,1)S(1)}, u32[]{:S(2)}, u32[]{:S(2)}) async-start(bf16[32,40,1024]{2,1,0:T(8,128)(2,1)} %param.6), calls=%async_computation | async-start | bytes 5242880 | tf_op jit(solution)/shard_map/all_to_all | solution.py:51
  16.9 299.8 %reduce-scatter.4.cloned.1.call-start = ((), (), s32[]{:S(2)}) async-start(), calls=%async_computation.5 | async-start | bytes 6758400 | tf_op jit(solution)/shard_map/reduce_scatter | solution.py:65
  101.6 3.9 copy-start
  101.6 3.9 copy-start.1
  102.0 7.7 %copy-start.2 = (f32[1280]{0:T(1024)S(1)}, f32[1280]{0:T(1024)}, u32[]{:S(2)}) copy-start(f32[1280]{0:T(1024)} %param.10) | copy-start | bytes 15364
  318.9 99.7 %all-to-all-start.2 = ((f32[8,40,1280]{2,1,0:T(8,128)}), f32[8,40,1280]{2,1,0:T(8,128)S(1)}, u32[]{:S(2)}, u32[]{:S(2)}) async-start(f32[8,40,1280]{2,1,0:T(8,128)} %broadcast_in_dim.26), calls=%async_computation.2 | async-start | bytes 3276800 | tf_op jit(solution)/shard_map/all_to_all | solution.py:20
Sparse Core Ops, SparseCore 0:
  9.8 84.4 all-gather.1
  140.7 163.7 reduce-scatter.3
where the time goes:
time: 433 us; the launch traced here: 427 us
  blocking collectives  238 us (55%)
  waiting for transfers between devices  77.4 us (18%)
  matrix products  31.1 us (7%)
  local copies, waits for them, and re-layouts  29.2 us (7%)
  other arithmetic  18.1 us (4%)
  between operations  17.3 us (4%)
  starting transfers between devices  16.6 us (4%)
    all_to_all x1, blocking collectives, shards(): lax.all_to_all(grad_image, MP, split_axis=1, concat_axis=0, tiled=True)  152 us
    psum x5, blocking collectives, by_axis(): return functools.reduce(lax.psum, axes, x)  85.3 us
    all_to_all x1, waiting for transfers between devices, shards(): lax.all_to_all(features, MP, split_axis=0, concat_axis=1, tiled=True)  72.1 us
    unnamed x8, local copies, waits for them, and re-layouts  14.3 us
    dot_general x1, matrix products, shards(): jnp.einsum('io,nos->nis', weight_full, grad_pre, preferred_element_type=j...  12.1 us
    dot_general x1, matrix products, shards(): jnp.einsum('nis,nos->io', image_block, grad_pre, preferred_element_type=j...  11.6 us
    transpose x1, local copies, waits for them, and re-layouts, shards(): jnp.einsum('io,nos->nis', weight_full, grad_pre, preferred_element_type=j...  11.6 us
    all_to_all x1, starting transfers between devices, shards(): lax.all_to_all(features, MP, split_axis=0, concat_axis=1, tiled=True)  9.01 us
  transfers between devices with their start and end apart: 4, of which 2 were waited for; matrix products, arithmetic and copies ran while one was open for 7% of the time, Pallas kernels for 0%

commit v1 on v0

--- a/solution.py
+++ b/solution.py
@@ -1,5 +1,3 @@
-import functools
-
 import jax
 import jax.numpy as jnp
 from jax import lax
@@ -22,10 +20,6 @@
 
 def taken_together(x, axis):
     return from_everyone(x, axis).sum(axis=0)
-
-
-def by_axis(x, axes):
-    return functools.reduce(lax.psum, axes, x)
 
 
 def head_total(pre, norm_gain, norm_bias, logit_vector, signs):
@@ -58,16 +52,17 @@
     grad_image = jnp.einsum(
         "io,nos->nis", weight_full, grad_pre, preferred_element_type=jnp.float32
     )
-    grad_features = lax.all_to_all(grad_image, MP, split_axis=1, concat_axis=0, tiled=True)
+    grad_features = lax.all_to_all(
+        grad_image.astype(jnp.bfloat16), MP, split_axis=1, concat_axis=0, tiled=True
+    ).astype(jnp.float32)
     weight_term = jnp.einsum(
         "nis,nos->io", image_block, grad_pre, preferred_element_type=jnp.float32
     )
     weight_rows = lax.psum_scatter(weight_term, MP, scatter_dimension=0, tiled=True)
     grad_weight = taken_together(weight_rows, DP)
-    total_sum, head_grads = (
-        by_axis(total, DP_MP),
-        by_axis(jnp.stack([grad_gain, grad_bias, grad_vec]), DP_MP),
-    )
+    small = jnp.stack([grad_gain, grad_bias, grad_vec, jnp.full_like(grad_gain, total)])
+    small = lax.psum(small, DP_MP)
+    total_sum, head_grads = small[3, 0], small[:3]
     image_total = pre.shape[0] * lax.axis_size(DP) * lax.axis_size(MP)
     loss = total_sum / image_total
     return (grad_features, grad_weight, head_grads, loss)

time: 433 us -> 426 us (0.984)
  blocking collectives: 238 us -> 181 us
  waiting for transfers between devices: 77.4 us -> 107 us
  other arithmetic: 18.1 us -> 38.1 us
  local copies, waits for them, and re-layouts: 29.2 us -> 34.1 us
    all_to_all x1, blocking collectives: 152 us -> 81.6 us  [shards(): lax.all_to_all(grad_image.astype(jnp.bfloat16), MP, split_axis=1, concat_...]
    reduce_scatter x1, waiting for transfers between devices: 0.01 us -> 29.9 us  [shards(): lax.psum_scatter(weight_term, MP, scatter_dimension=0, tiled=True)]
    unnamed x0 -> x1, other arithmetic: none -> 15.6 us
    psum x5 -> x1, blocking collectives: 85.3 us -> 99.4 us  [shards(): small = lax.psum(small, DP_MP)]
    transpose x1 -> x0, local copies, waits for them, and re-layouts: 11.6 us -> none  [shards(): jnp.einsum('io,nos->nis', weight_full, grad_pre, preferred_element_type=j...]
    convert_element_type x0 -> x1, local copies, waits for them, and re-layouts: none -> 7.87 us  [shards(): grad_image.astype(jnp.bfloat16)]
    unnamed x8 -> x12, local copies, waits for them, and re-layouts: 14.3 us -> 18.8 us
  transfers between devices with their start and end apart: 4 -> 4, of which waited for: 2 -> 3; matrix products, arithmetic and copies ran while one was open for 7% -> 12% of each run, Pallas kernels for 0% -> 0%
where the time goes in v1:
time: 426 us; the launch traced here: 422 us
  blocking collectives  181 us (42%)
  waiting for transfers between devices  107 us (25%)
  other arithmetic  38.1 us (9%)
  local copies, waits for them, and re-layouts  34.1 us (8%)
  matrix products  28.7 us (7%)
  between operations  17.3 us (4%)
  starting transfers between devices  15.6 us (4%)
    psum x1, blocking collectives, shards(): small = lax.psum(small, DP_MP)  99.4 us
    all_to_all x1, blocking collectives, shards(): lax.all_to_all(grad_image.astype(jnp.bfloat16), MP, split_axis=1, concat_...  81.6 us
    all_to_all x1, waiting for transfers between devices, shards(): lax.all_to_all(features, MP, split_axis=0, concat_axis=1, tiled=True)  72.1 us
    reduce_scatter x1, waiting for transfers between devices, shards(): lax.psum_scatter(weight_term, MP, scatter_dimension=0, tiled=True)  29.9 us
    unnamed x12, local copies, waits for them, and re-layouts  18.8 us
    unnamed x1, other arithmetic  15.6 us
    dot_general x1, matrix products, shards(): jnp.einsum('nis,nos->io', image_block, grad_pre, preferred_element_type=j...  11.6 us
    dot_general x1, matrix products, shards(): jnp.einsum('io,nos->nis', weight_full, grad_pre, preferred_element_type=j...  9.76 us
  transfers between devices with their start and end apart: 4, of which 3 were waited for; matrix products, arithmetic and copies ran while one was open for 12% of the time, Pallas kernels for 0%

profile of v1, /device:TPU:6, one launch (start us, length us, event | category | flops | bytes accessed | tf_op | source)
XLA Modules:
  0.0 422.1 jit_solution(12105964118553905364)
XLA Ops:
  7.2 0.7 all-gather.2.cloned.1.call-update
  7.9 9.0 %all-to-all-start = ((bf16[32,40,1024]{2,1,0:T(8,128)(2,1)}), bf16[32,40,1024]{2,1,0:T(8,128)(2,1)S(1)}, u32[]{:S(2)}, u32[]{:S(2)}) async-start(bf16[32,40,1024]{2,1,0:T(8,128)(2,1)} %param.6), calls=%async_computation | async-start | bytes 5242880 | tf_op jit(solution)/shard_map/all_to_all | solution.py:45
  16.9 0.0 reduce-scatter.4.cloned.1.call-start
  17.6 72.1 %all-to-all-done = bf16[32,40,1024]{2,1,0:T(8,128)(2,1)S(1)} async-done(((bf16[32,40,1024]{2,1,0:T(8,128)(2,1)}), bf16[32,40,1024]{2,1,0:T(8,128)(2,1)S(1)}, u32[]{:S(2)}, u32[]{:S(2)}) %all-to-all-start) | async-done | bytes 2621472 | tf_op jit(solution)/shard_map/all_to_all | solution.py:45
  89.7 4.6 %all-gather.2.cloned.1.call-done = bf16[1280,1280]{1,0:T(8,128)(2,1)} async-done(((bf16[40,1280]{1,0:T(8,128)(2,1)}), bf16[1280,1280]{1,0:T(8,128)(2,1)}) %all-gather.2.cloned.1.call-update) | async-done | bytes 3276816 | tf_op jit(solution)/shard_map/all_gather | solution.py:44
  94.3 7.3 %fusion.11 = (f32[1280]{0:T(1024)S(1)}, f32[1024,1280]{1,0:T(8,128)}) fusion(bf16[1280,1024]{1,0:T(8,128)(2,1)S(1)} %bitcast.93, bf16[1280,1280]{1,0:T(8,128)(2,1)} %all-gather.2.cloned.1.call-done), kind=kOutput, calls=%fused_computation.31 | convolution fusion | flops 3356752640 | bytes 11146240 | tf_op jit(solution)/shard_map/io,nis->nos/dot_general | solution.py:46
  101.6 0.1 reduce_sum.147
  101.7 0.1 reduce_sum.148
  101.8 0.1 sub.52
  101.9 0.1 sub.53
  102.0 3.1 fusion.2
  105.1 0.1 reduce_sum.150
  105.2 0.1 reduce_sum.151
  105.3 0.1 mul.155
  105.4 0.1 mul.156
  105.5 4.2 multiply_reduce_fusion.1
  109.7 0.6 multiply_reduce_fusion.3
  111.0 5.7 %multiply_reduce_fusion = (f32[1280]{0:T(1024)S(1)}, f32[1280]{0:T(1024)S(1)}, f32[1280]{0:T(1024)S(1)}, f32[1280]{0:T(1024)S(1)}) fusion(f32[1024,1280]{1,0:T(8,128)} %get-tuple-element.13, f32[1280]{0:T(1024)S(1)} %mul.156, f32[1280]{0:T(1024)S(1)} %sub.53, f32[1280]{0:T(1024)S(1)} %copy-done, f32[1280]{0:T(1024)S(1)} %copy-done.1, ...), kind=kLoop, calls=%fused_computation.11 | loop fusion | flops 27520000 | bytes 5288960 | tf_op jit(solution)/shard_map/transpose(jvp())/reduce_sum | solution.py:33
  116.7 0.1 reduce_sum.157
  116.8 0.1 reduce_sum.158
  116.9 0.1 reduce_sum.154
  117.0 0.1 reduce_sum.155
  117.1 0.1 mul.177
  117.2 0.1 mul.178
  117.3 3.1 fusion.4
  120.4 0.1 reduce_sum.160
  120.5 0.1 reduce_sum.161
  120.6 0.1 broadcast_in_dim.11
  120.7 0.1 broadcast_in_dim.24
  120.8 11.6 %convolution_bitcast_fusion = f32[1280,1280]{0,1:T(8,128)} fusion(bf16[1280,1024]{1,0:T(8,128)(2,1)S(1)} %bitcast.94, f32[1024,1280]{1,0:T(8,128)} %get-tuple-element.13, f32[1280]{0:T(1024)S(1)} %broadcast_in_dim.24, f32[1280]{0:T(1024)S(1)} %mul.178, f32[1280]{0:T(1024)S(1)} %copy-done.1, f32[1280]{0:T(1024)S(1)} %mul.156, f32[1280]{0:T(1024)S(1)} %sub.53, ...), kind=kOutput, calls=%fused_computation | convolution fusion | flops 3380346880 | bytes 14453760 | tf_op jit(solution)/shard_map/nis,nos->io/dot_general | solution.py:58
  132.4 8.2 %copy.22 = f32[1280,1280]{1,0:T(8,128)} copy(f32[1280,1280]{0,1:T(8,128)} %convolution_bitcast_fusion) | data formatting | bytes 13107200
  140.6 9.8 %fusion.5 = bf16[1,1280,1024]{1,2,0:T(8,128)(2,1)S(1)} fusion(bf16[1280,1280]{1,0:T(8,128)(2,1)} %all-gather.2.cloned.1.call-done, f32[1024,1280]{1,0:T(8,128)} %get-tuple-element.13, f32[1280]{0:T(1024)S(1)} %broadcast_in_dim.24, f32[1280]{0:T(1024)S(1)} %mul.178, f32[1280]{0:T(1024)S(1)} %copy-done.1, f32[1280]{0:T(1024)S(1)} %mul.156, ...), kind=kOutput, calls=%fused_computation.19 | convolution fusion | flops 3381657600 | bytes 11176960 | tf_op jit(solution)/shard_map/io,nos->nis/dot_general | solution.py:52
  150.4 7.9 %copy.17 = bf16[1,1280,1024]{2,0,1:T(2,128)(2,1)} copy(bf16[1,1280,1024]{1,2,0:T(8,128)(2,1)S(1)} %fusion.5) | data formatting | bytes 5242880 | tf_op jit(solution)/shard_map/convert_element_type | solution.py:56
  158.2 0.5 broadcast.211
  158.8 15.6 %reduce.26 = bf16[1280,1024]{1,0:T(8,128)(2,1)S(1)} reduce(bf16[1280,1,1024]{2,1,0:T(2,128)(2,1)} %bitcast.90, bf16[]{:T(256)} %broadcast.211), dimensions={1}, to_apply=%bitcast.83.reduce_sub_computation | reduce | bytes 5242882
  174.3 2.9 reshape.373
  177.3 81.6 %all_to_all.23 = bf16[32,2,20480]{2,1,0:T(2,128)(2,1)S(1)} all-to-all(bf16[32,2,20480]{2,1,0:T(2,128)(2,1)} %reshape.373), channel_id=1, replica_groups=mesh['dp_0'=4,'dp_1'=2,'mp_0'=4,'mp_1'=4,'mp_2'=2] {'mp_0','mp_1','mp_2'}, dimensions={0} | all-to-all | bytes 5242880 | tf_op jit(solution)/shard_map/all_to_all | solution.py:55
  258.8 29.9 %reduce-scatter.4.cloned.1.call-done = f32[40,1280]{1,0:T(8,128)} async-done(((f32[1280,1280]{1,0:T(8,128)}), f32[40,1280]{1,0:T(8,128)}) %reduce-scatter.4.cloned.1.call-update) | async-done | bytes 204816 | tf_op jit(solution)/shard_map/reduce_scatter | solution.py:61
  288.7 2.2 broadcast_in_dim.26
  291.0 6.5 %all-to-all-start.2 = ((f32[8,40,1280]{2,1,0:T(8,128)}), f32[8,40,1280]{2,1,0:T(8,128)}, u32[]{:S(2)}, u32[]{:S(2)}) async-start(f32[8,40,1280]{2,1,0:T(8,128)} %broadcast_in_dim.26), calls=%async_computation.2 | async-start | bytes 3276800 | tf_op jit(solution)/shard_map/all_to_all | solution.py:18
  297.5 0.1 pad.3.clone
  297.6 0.1 maximum_maximum_fusion
  297.7 99.4 %psum.7 = f32[4,1280]{1,0:T(4,128)S(1)} all-reduce(f32[4,1280]{1,0:T(4,128)S(1)} %maximum_maximum_fusion), channel_id=1, replica_groups=mesh['dp_0'=4,'dp_1'=2,'mp_0'=4,'mp_1'=4,'mp_2'=2] {'dp_0','dp_1','mp_0'..., use_global_device_ids=true, to_apply=%region_15.16 | all-reduce | flops 5120 | bytes 40960 | tf_op jit(solution)/shard_map/psum | solution.py:64
  397.0 0.5 slice.9
  398.2 7.2 %reshape.374 = bf16[1280,1,1024]{2,1,0:T(2,128)(2,1)} reshape(bf16[32,2,20480]{2,1,0:T(2,128)(2,1)S(1)} %all_to_all.23) | data formatting | bytes 5242880
  405.4 3.5 copy.18
  408.9 3.0 convert.1
  411.9 2.2 reduce_sum.162
  (20 shorter events, 0.1 us)
Async XLA Ops:
  7.2 87.1 %all-gather.2.cloned.1.call-start = ((), (), s32[]{:S(2)}) async-start(), calls=%async_computation.4 | async-start | bytes 3379200 | tf_op jit(solution)/shard_map/all_gather | solution.py:44
  7.9 81.8 %all-to-all-start = ((bf16[32,40,1024]{2,1,0:T(8,128)(2,1)}), bf16[32,40,1024]{2,1,0:T(8,128)(2,1)S(1)}, u32[]{:S(2)}, u32[]{:S(2)}) async-start(bf16[32,40,1024]{2,1,0:T(8,128)(2,1)} %param.6), calls=%async_computation | async-start | bytes 5242880 | tf_op jit(solution)/shard_map/all_to_all | solution.py:45
  16.9 271.8 %reduce-scatter.4.cloned.1.call-start = ((), (), s32[]{:S(2)}) async-start(), calls=%async_computation.5 | async-start | bytes 6758400 | tf_op jit(solution)/shard_map/reduce_scatter | solution.py:61
  101.6 3.9 copy-start
  101.6 3.9 copy-start.1
  102.0 7.7 %copy-start.2 = (f32[1280]{0:T(1024)S(1)}, f32[1280]{0:T(1024)}, u32[]{:S(2)}) copy-start(f32[1280]{0:T(1024)} %param.10) | copy-start | bytes 15364
  291.0 120.9 %all-to-all-start.2 = ((f32[8,40,1280]{2,1,0:T(8,128)}), f32[8,40,1280]{2,1,0:T(8,128)}, u32[]{:S(2)}, u32[]{:S(2)}) async-start(f32[8,40,1280]{2,1,0:T(8,128)} %broadcast_in_dim.26), calls=%async_computation.2 | async-start | bytes 3276800 | tf_op jit(solution)/shard_map/all_to_all | solution.py:18
  397.0 11.9 %copy-start.3 = (f32[4,1280]{1,0:T(4,128)}, f32[4,1280]{1,0:T(4,128)S(1)}, u32[]{:S(2)}) copy-start(f32[4,1280]{1,0:T(4,128)S(1)} %psum.7) | copy-start | bytes 61444
Sparse Core Ops, SparseCore 0:
  9.8 84.4 all-gather.1
  140.7 147.9 reduce-scatter.3
